TPU v7x, 32 devices: a whole 2x2x4 slice. The times are simulated.
32 devices in a mesh: groups: 2 (over y), frames: 4 (over z), code: 2 (over x), head: 2 (over core).
Axes of the slice: x: 2, y: 2, z: 4, core: 2. Of those that a mesh axis runs over, the one named last changes fastest.
Arguments:
- video: bfloat16 [256, 16, 1024], P(('code', 'head'), ('groups', 'frames')), parts along dimension 1, may hold values from -6 to 6
- conv_weight: bfloat16 [3, 1024, 1024], replicated, may hold values from -0.109375 to 0.109375
- norm_gain: float32 [1024], replicated, may hold values from 0.1 to 1.9
- qkv_weight: bfloat16 [1024, 3, 1024], P(None, None, ('code', 'head')), may hold values from -1 to 1
- out_weight: bfloat16 [1024, 1024], P(('code', 'head')), may hold values from -0.1875 to 0.1875
- latent_weight: bfloat16 [1024, 16], replicated, may hold values from -0.1875 to 0.1875
- codebook: bfloat16 [16, 65536], P(None, ('code', 'head')), may hold values from -9 to 9
- reference_codes: int32 [256, 16], P(None, ('groups', 'frames')), parts along dimension 1, may hold values from 0 to 65535
Outputs:
- encoded: bfloat16 [256, 16, 1024], P(('code', 'head'), ('groups', 'frames')), parts along dimension 1
- nearest_distance: float32 [256, 16], P(('code', 'head'), ('groups', 'frames')), parts along dimension 1
- reference_gap: float32 [256, 16], P(('code', 'head'), ('groups', 'frames')), parts along dimension 1
There are 2 independent parts, one for each index of `groups`. A program takes and returns all parts, laid end to end along the dimension named above; an argument that names none is the same for every part. Nothing has to cross between parts.
All inputs are finite; a program needn't handle non-finite values.
Results may differ from a plain program's by a relative error of at most 0.015.
Values may be sent and summed in bfloat16 or wider, within the bound.
No kernel may reach another device: no remote copies, remote signals or barrier semaphores. Data moves between devices by JAX's collectives and lax.ppermute only.
A program may use at most 64 MiB of HBM per device.

v0:
```python
import math

import jax
import jax.numpy as jnp
from jax import lax
from jax.sharding import PartitionSpec as P

HEADS = 16


EPSILON = 1e-06


def passed_along(block, axis, distance):
    devices = range(lax.axis_size(axis))
    route = [(i - distance, i) for i in devices if i - distance in devices]
    return lax.ppermute(block, axis, route)


def merged(value, axis, combine):
    everything = jax.tree.map(lambda part: lax.all_gather(part, axis), value)
    leading = jax.tree.map(lambda part: part[0], everything)

    def lap(k, so_far):
        return combine(so_far, jax.tree.map(lambda part: part[k], everything))

    return lax.fori_loop(1, lax.axis_size(axis), lap, leading)


def normalize(block_input, norm_gain):
    values32 = block_input.astype(jnp.float32)
    mean_square = jnp.mean(values32 * values32, axis=-1, keepdims=True)
    return (values32 * lax.rsqrt(mean_square + EPSILON) * norm_gain).astype(jnp.bfloat16)


def attend_slab(queries, query_frame, keys, values, frames_here, local_heads, head_dim):
    slab_rows = queries.shape[0]
    query_heads = queries.reshape(slab_rows, local_heads, head_dim)
    score_scale = 1.0 / math.sqrt(head_dim)
    latest = jnp.max(query_frame)
    start_state = (
        jnp.full((slab_rows, local_heads), -1e30, jnp.float32),
        jnp.zeros((slab_rows, local_heads), jnp.float32),
        jnp.zeros((slab_rows, local_heads, head_dim), jnp.float32),
    )
    running = start_state
    key_part = lax.all_gather(keys, "frames", axis=0, tiled=True)
    value_part = lax.all_gather(values, "frames", axis=0, tiled=True)
    length = key_part.shape[0]
    block = math.gcd(length, slab_rows)
    count = length // block
    key_blocks = key_part.reshape(count, block, local_heads, head_dim)
    value_blocks = value_part.reshape(count, block, local_heads, head_dim)

    def absorb_visit(state, operands):
        key_block, value_block, block_index = operands
        first_row = block_index * block

        def compute(current):
            highest, denominator, summed = current
            key_rows = first_row + jnp.arange(block, dtype=jnp.int32)
            key_frame = key_rows // slab_rows * frames_here + key_rows % frames_here
            allowed = (key_frame[None, :] <= query_frame[:, None])[:, None, :]
            scores = (
                jnp.einsum(
                    "qhd,khd->qhk", query_heads, key_block, preferred_element_type=jnp.float32
                )
                * score_scale
            )
            scores = jnp.where(allowed, scores, -1e30)
            fresh = jnp.maximum(highest, jnp.max(scores, axis=2))
            weights = jnp.where(allowed, jnp.exp(scores - fresh[:, :, None]), 0.0)
            factor = jnp.exp(highest - fresh)
            denominator = denominator * factor + jnp.sum(weights, axis=2)
            summed = summed * factor[:, :, None] + jnp.einsum(
                "qhk,khd->qhd",
                weights.astype(jnp.bfloat16),
                value_block,
                preferred_element_type=jnp.float32,
            )
            return (fresh, denominator, summed)

        earliest = first_row // slab_rows * frames_here
        state = lax.cond(earliest <= latest, compute, lambda kept: kept, state)
        return (state, None)

    running, unused = lax.scan(
        absorb_visit, running, (key_blocks, value_blocks, jnp.arange(count, dtype=jnp.int32))
    )
    highest, denominator, summed = running
    return (
        (summed / denominator[:, :, None])
        .reshape(slab_rows, local_heads * head_dim)
        .astype(jnp.bfloat16)
    )


def scan_codes(running, latent_t, codes, offset, wanted):
    code_dim, length = codes.shape
    block = math.gcd(length, 4096)
    count = length // block
    latent32 = latent_t.astype(jnp.float32)
    squares = jnp.sum(latent32 * latent32, axis=0)
    code_blocks = jnp.transpose(codes.reshape(code_dim, count, block), (1, 0, 2))

    def scan_visit(state, operands):
        least, chosen = state
        code_block, block_index = operands
        codes32 = code_block.astype(jnp.float32)
        code_squares = jnp.sum(codes32 * codes32, axis=0)
        dots = lax.dot_general(
            latent_t, code_block, (((0,), (0,)), ((), ())), preferred_element_type=jnp.float32
        )
        distance = (squares[:, None] - 2.0 * dots + code_squares[None, :]) / code_dim
        labels = offset + block_index * block + jnp.arange(block, dtype=jnp.int32)
        least = jnp.minimum(least, jnp.min(distance, axis=1))
        chosen = chosen + jnp.sum(
            jnp.where(labels[None, :] == wanted[:, None], distance, 0.0), axis=1
        )
        return ((least, chosen), None)

    running, unused = lax.scan(
        scan_visit, running, (code_blocks, jnp.arange(count, dtype=jnp.int32))
    )
    return running


def empty_state(count):
    return (jnp.full((count,), 1e30, jnp.float32), jnp.zeros((count,), jnp.float32))


def combine_minima(first, second):
    return (jnp.minimum(first[0], second[0]), first[1] + second[1])


def shards(
    video, conv_weight, norm_gain, qkv_weight, out_weight, latent_weight, codebook, reference_codes
):
    positions, frames_here, model_width = video.shape
    own_rows = positions * frames_here
    earlier = passed_along(video, "frames", 1)
    padded = jnp.concatenate([earlier, video], axis=1)
    stacked = jnp.concatenate([padded[:, 2:], padded[:, 1:-1], padded[:, :-2]], axis=2)
    mixed = jnp.dot(
        stacked.reshape(own_rows, 3 * model_width),
        conv_weight.reshape(3 * model_width, model_width),
        preferred_element_type=jnp.float32,
    )
    block_input = (
        video.reshape(own_rows, model_width).astype(jnp.float32) + jax.nn.silu(mixed)
    ).astype(jnp.bfloat16)
    normed = normalize(block_input, norm_gain)
    local_width = qkv_weight.shape[2]
    projection = qkv_weight.reshape(model_width, 3 * local_width)
    triple = jnp.dot(
        lax.all_gather(normed, ("code", "head"), axis=0, tiled=True),
        projection,
        preferred_element_type=jnp.float32,
    ).astype(jnp.bfloat16)
    queries = triple[:, :local_width]
    keys = triple[:, local_width : 2 * local_width]
    values = triple[:, 2 * local_width :]
    slab_rows = triple.shape[0]
    head_dim = model_width // HEADS
    local_heads = local_width // head_dim
    slab_index = lax.axis_index("frames")
    local_frame = jnp.arange(slab_rows, dtype=jnp.int32) % frames_here
    query_frame = slab_index * frames_here + local_frame
    attended = attend_slab(queries, query_frame, keys, values, frames_here, local_heads, head_dim)
    projected = lax.psum_scatter(
        jnp.dot(attended, out_weight, preferred_element_type=jnp.float32).astype(jnp.bfloat16),
        ("code", "head"),
        scatter_dimension=0,
        tiled=True,
    ).astype(jnp.float32)
    encoded_rows = (block_input.astype(jnp.float32) + projected).astype(jnp.bfloat16)
    encoded = encoded_rows.reshape(positions, frames_here, model_width)
    latent_t = lax.dot_general(
        latent_weight, encoded_rows, (((0,), (1,)), ((), ())), preferred_element_type=jnp.float32
    ).astype(jnp.bfloat16)
    group_index = lax.axis_index(("code", "head"))
    wanted_all = reference_codes.reshape(-1)
    every_latent = lax.all_gather(latent_t, ("code", "head"), axis=1, tiled=True)
    shard_codes = codebook.shape[1]
    partial_state = scan_codes(
        empty_state(every_latent.shape[1]),
        every_latent,
        codebook,
        group_index * shard_codes,
        wanted_all,
    )
    merged_least, merged_chosen = merged(partial_state, ("code", "head"), combine_minima)
    least = lax.dynamic_slice_in_dim(merged_least, group_index * own_rows, own_rows, 0)
    chosen = lax.dynamic_slice_in_dim(merged_chosen, group_index * own_rows, own_rows, 0)
    return (
        encoded,
        least.reshape(positions, frames_here),
        (chosen - least).reshape(positions, frames_here),
    )


def solution(mesh):
    return jax.shard_map(
        shards,
        mesh=mesh,
        in_specs=(
            P(("code", "head"), ("groups", "frames"), None),
            P(),
            P(),
            P(None, None, ("code", "head")),
            P(("code", "head"), None),
            P(),
            P(None, ("code", "head")),
            P(None, ("groups", "frames")),
        ),
        out_specs=(
            P(("code", "head"), ("groups", "frames"), None),
            P(("code", "head"), ("groups", "frames")),
            P(("code", "head"), ("groups", "frames")),
        ),
        check_vma=False,
    )
```

profile of v0, /device:TPU:24, one launch (start us, length us, event | category | flops | bytes accessed | tf_op | source)
XLA Modules:
  0.0 230.3 jit_solution(13557342944345085490)
XLA Ops:
  9.7 7.8 %collective-permute-done = bf16[64,2,1024]{2,1,0:T(2,128)(2,1)S(1)} collective-permute-done((bf16[64,2,1024]{2,1,0:T(2,128)(2,1)}, bf16[64,2,1024]{2,1,0:T(2,128)(2,1)S(1)}, u32[]{:S(2)}, u32[]{:S(2)}) %collective-permute-start) | collective-permute-done | bytes 262176 | tf_op jit(solution)/shard_map/ppermute | solution.py:17
  20.9 4.3 %fusion.37 = (f32[128]{0:T(128)S(1)}, bf16[128,1024]{1,0:T(8,128)(2,1)S(1)}) fusion(f32[128,1024]{1,0:T(8,128)S(1)} %reshape.130, bf16[128,3072]{1,0:T(8,128)(2,1)} %reshape.120, bf16[3072,1024]{1,0:T(8,128)(2,1)} %bitcast.105), kind=kOutput, calls=%fused_computation.62 | convolution fusion | flops 806485888 | bytes 7864832 | tf_op jit(solution)/shard_map/dot_general | solution.py:144
  27.9 16.0 %all-gather.8.cloned.1.call-done = bf16[512,1024]{1,0:T(8,128)(2,1)} async-done(((bf16[128,1024]{1,0:T(8,128)(2,1)}), bf16[512,1024]{1,0:T(8,128)(2,1)}) %all-gather.8.cloned.1.call-update) | async-done | bytes 1048592 | tf_op jit(solution)/shard_map/all_gather | solution.py:156
  43.9 2.7 %convolution_convert_fusion.1 = bf16[512,768]{1,0:T(8,128)(2,1)S(1)} fusion(bf16[512,1024]{1,0:T(8,128)(2,1)} %all-gather.8.cloned.1.call-done, bf16[1024,768]{0,1:T(8,128)(2,1)} %bitcast.95), kind=kOutput, calls=%fused_computation.53 | convolution fusion | flops 805699584 | bytes 3407872 | tf_op jit(solution)/shard_map/dot_general | solution.py:155
  49.4 24.8 %all-gather.10.cloned.1.call-done = bf16[2048,256]{1,0:T(8,128)(2,1)} async-done(((bf16[512,256]{1,0:T(8,128)(2,1)}), bf16[2048,256]{1,0:T(8,128)(2,1)}) %all-gather.10.cloned.1.call-update) | async-done | bytes 1048592 | tf_op jit(solution)/shard_map/all_gather | solution.py:47
  74.2 3.3 %reshape.145 = bf16[4,512,4,64]{3,2,1,0:T(4,128)(2,1)S(1)} reshape(bf16[2048,256]{1,0:T(8,128)(2,1)} %all-gather.10.cloned.1.call-done) | data formatting | bytes 2097152 | tf_op jit(solution)/shard_map/reshape | solution.py:52
  77.5 2.3 %copy.33 = bf16[4,512,4,64]{1,3,2,0:T(8,128)(2,1)} copy(bf16[4,512,4,64]{3,2,1,0:T(4,128)(2,1)S(1)} %reshape.145) | data formatting | bytes 2097152
  79.8 23.3 %all-gather.12.cloned.1.call-done = bf16[2048,256]{1,0:T(8,128)(2,1)} async-done(((bf16[512,256]{1,0:T(8,128)(2,1)}), bf16[2048,256]{1,0:T(8,128)(2,1)}) %all-gather.12.cloned.1.call-update) | async-done | bytes 1048592 | tf_op jit(solution)/shard_map/all_gather | solution.py:48
  103.2 3.3 %reshape.146 = bf16[4,512,4,64]{3,2,1,0:T(4,128)(2,1)S(1)} reshape(bf16[2048,256]{1,0:T(8,128)(2,1)} %all-gather.12.cloned.1.call-done) | data formatting | bytes 2097152 | tf_op jit(solution)/shard_map/reshape | solution.py:53
  106.5 2.4 %copy.34 = bf16[4,512,4,64]{1,3,2,0:T(8,128)(2,1)} copy(bf16[4,512,4,64]{3,2,1,0:T(4,128)(2,1)S(1)} %reshape.146) | data formatting | bytes 2097152
  108.9 30.0 %while.49 = (s32[]{:T(128)}, f32[512,4]{0,1:T(4,128)S(1)}, f32[512,4]{0,1:T(4,128)S(1)}, f32[512,4,64]{0,2,1:T(8,128)S(1)}, s32[4]{0:T(128)S(1)}, /*index=5*/s32...) while((s32[]{:T(128)}, f32[512,4]{0,1:T(4,128)S(1)}, ...), condition=%wide.region_7.8_spmd.clone, body=%wide.region_2.7_spmd.clone.sunk | while | flops 282612256 | bytes 15621669 | solution.py:87
  110.9 5.5 %conditional.3 = ((f32[512,4]{0,1:T(4,128)S(1)}, f32[512,4]{0,1:T(4,128)S(1)}, f32[512,4,64]{0,2,1:T(8,128)S(1)})) conditional(s32[]{:T(128)} %convert_element_type.108, (f32[512,4]{0,1:T(4,128)S(1)}, f32[512,4]{0,1:T(4,128)S(1)}, f32[512,4,64]{0,2,1:T(8,128)S(1)}) %tuple.127, (s32[]{:T(128)}, s32[]{:T(128)}, bf16[4,512,4,64]{1,3,2,0:T(8,128)(2,1)}, ...), branch_computations={%region_3.3_spmd, %region_4.6_spmd.clone} | conditional | flops 282611712 | bytes 15617068 | solution.py:84
  114.1 2.3 %fusion.15 = f32[512,4,64]{0,2,1:T(8,128)S(1)} fusion(f32[4,512,512]{2,1,0:T(8,128)S(1)} %get-tuple-element.626, f32[512,4]{0,1:T(4,128)S(1)} %max.5, pred[512,512]{0,1:T(8,128)(4,1)S(1)} %broadcast_compare_fusion, f32[512,4,64]{0,2,1:T(8,128)S(1)} %get-tuple-element.540, bf16[4,512,4,64]{1,3,2,0:T(8,128)(2,1)} %get-tuple-element.541, ...), kind=kOutput, calls=%fused_computation.21 | convolution fusion | flops 139722752 | bytes 5784064 | tf_op jit(solution)/shard_map/while/body/eval_jaxpr/cond/branch_1_fun/qhk,khd->qhd/dot_general | solution.py:75
  118.4 5.5 %conditional.3 = ((f32[512,4]{0,1:T(4,128)S(1)}, f32[512,4]{0,1:T(4,128)S(1)}, f32[512,4,64]{0,2,1:T(8,128)S(1)})) conditional(s32[]{:T(128)} %convert_element_type.108, (f32[512,4]{0,1:T(4,128)S(1)}, f32[512,4]{0,1:T(4,128)S(1)}, f32[512,4,64]{0,2,1:T(8,128)S(1)}) %tuple.127, (s32[]{:T(128)}, s32[]{:T(128)}, bf16[4,512,4,64]{1,3,2,0:T(8,128)(2,1)}, ...), branch_computations={%region_3.3_spmd, %region_4.6_spmd.clone} | conditional | flops 282611712 | bytes 15617068 | solution.py:84
  121.6 2.3 %fusion.15 = f32[512,4,64]{0,2,1:T(8,128)S(1)} fusion(f32[4,512,512]{2,1,0:T(8,128)S(1)} %get-tuple-element.626, f32[512,4]{0,1:T(4,128)S(1)} %max.5, pred[512,512]{0,1:T(8,128)(4,1)S(1)} %broadcast_compare_fusion, f32[512,4,64]{0,2,1:T(8,128)S(1)} %get-tuple-element.540, bf16[4,512,4,64]{1,3,2,0:T(8,128)(2,1)} %get-tuple-element.541, ...), kind=kOutput, calls=%fused_computation.21 | convolution fusion | flops 139722752 | bytes 5784064 | tf_op jit(solution)/shard_map/while/body/eval_jaxpr/cond/branch_1_fun/qhk,khd->qhd/dot_general | solution.py:75
  125.9 5.5 %conditional.3 = ((f32[512,4]{0,1:T(4,128)S(1)}, f32[512,4]{0,1:T(4,128)S(1)}, f32[512,4,64]{0,2,1:T(8,128)S(1)})) conditional(s32[]{:T(128)} %convert_element_type.108, (f32[512,4]{0,1:T(4,128)S(1)}, f32[512,4]{0,1:T(4,128)S(1)}, f32[512,4,64]{0,2,1:T(8,128)S(1)}) %tuple.127, (s32[]{:T(128)}, s32[]{:T(128)}, bf16[4,512,4,64]{1,3,2,0:T(8,128)(2,1)}, ...), branch_computations={%region_3.3_spmd, %region_4.6_spmd.clone} | conditional | flops 282611712 | bytes 15617068 | solution.py:84
  129.1 2.3 %fusion.15 = f32[512,4,64]{0,2,1:T(8,128)S(1)} fusion(f32[4,512,512]{2,1,0:T(8,128)S(1)} %get-tuple-element.626, f32[512,4]{0,1:T(4,128)S(1)} %max.5, pred[512,512]{0,1:T(8,128)(4,1)S(1)} %broadcast_compare_fusion, f32[512,4,64]{0,2,1:T(8,128)S(1)} %get-tuple-element.540, bf16[4,512,4,64]{1,3,2,0:T(8,128)(2,1)} %get-tuple-element.541, ...), kind=kOutput, calls=%fused_computation.21 | convolution fusion | flops 139722752 | bytes 5784064 | tf_op jit(solution)/shard_map/while/body/eval_jaxpr/cond/branch_1_fun/qhk,khd->qhd/dot_general | solution.py:75
  133.4 5.5 %conditional.3 = ((f32[512,4]{0,1:T(4,128)S(1)}, f32[512,4]{0,1:T(4,128)S(1)}, f32[512,4,64]{0,2,1:T(8,128)S(1)})) conditional(s32[]{:T(128)} %convert_element_type.108, (f32[512,4]{0,1:T(4,128)S(1)}, f32[512,4]{0,1:T(4,128)S(1)}, f32[512,4,64]{0,2,1:T(8,128)S(1)}) %tuple.127, (s32[]{:T(128)}, s32[]{:T(128)}, bf16[4,512,4,64]{1,3,2,0:T(8,128)(2,1)}, ...), branch_computations={%region_3.3_spmd, %region_4.6_spmd.clone} | conditional | flops 282611712 | bytes 15617068 | solution.py:84
  136.6 2.3 %fusion.15 = f32[512,4,64]{0,2,1:T(8,128)S(1)} fusion(f32[4,512,512]{2,1,0:T(8,128)S(1)} %get-tuple-element.626, f32[512,4]{0,1:T(4,128)S(1)} %max.5, pred[512,512]{0,1:T(8,128)(4,1)S(1)} %broadcast_compare_fusion, f32[512,4,64]{0,2,1:T(8,128)S(1)} %get-tuple-element.540, bf16[4,512,4,64]{1,3,2,0:T(8,128)(2,1)} %get-tuple-element.541, ...), kind=kOutput, calls=%fused_computation.21 | convolution fusion | flops 139722752 | bytes 5784064 | tf_op jit(solution)/shard_map/while/body/eval_jaxpr/cond/branch_1_fun/qhk,khd->qhd/dot_general | solution.py:75
  141.6 24.8 %reduce-scatter.2.cloned.1.call-done = bf16[128,1024]{1,0:T(8,128)(2,1)} async-done(((bf16[512,1024]{1,0:T(8,128)(2,1)}), bf16[128,1024]{1,0:T(8,128)(2,1)}) %reduce-scatter.2.cloned.1.call-update) | async-done | bytes 262160 | tf_op jit(solution)/shard_map/reduce_scatter | solution.py:170
  167.6 5.2 %all_gather.27 = bf16[16,512]{1,0:T(8,128)(2,1)S(1)} all-gather(bf16[16,128]{1,0:T(8,128)(2,1)S(1)} %fusion.34), channel_id=1, replica_groups=mesh['groups'=2,'frames'=4,'code'=2,'head'=2] {'code','head'}, dimensions={1}, use_global_device_ids=true | all-gather | bytes 20480 | tf_op jit(solution)/shard_map/all_gather | solution.py:183
  172.8 37.9 %while.50 = (s32[]{:T(128)}, f32[512]{0:T(512)S(1)}, f32[512]{0:T(512)S(1)}, f32[512]{0:T(512)S(1)}, bf16[4,16,4096]{2,1,0:T(8,128)(2,1)S(1)}, /*index=5*/bf16[1...) while((s32[]{:T(128)}, f32[512]{0:T(512)S(1)}, ...), condition=%wide.wide.region_14.15_spmd.clone, body=%wide.wide.region_10.14_spmd.clone.sunk | while | flops 84083712 | bytes 17141940 | solution.py:122
  172.9 4.2 %fusion.65 = (f32[512]{0:T(512)S(1)}, f32[4096,512]{1,0:T(8,128)}) fusion(f32[4096]{0:T(1024)S(1)} %multiply_reduce_fusion.4, bf16[16,512]{1,0:T(8,128)(2,1)S(1)} %get-tuple-element.931, bf16[4,16,4096]{2,1,0:T(8,128)(2,1)S(1)} %get-tuple-element.930, s32[]{:T(128)} %get-tuple-element.913, f32[512]{0:T(512)S(1)} %get-tuple-element.929), kind=kOutput, calls=%fused_computation.80.clone.clone.1 | convolution fusion | flops 77594112 | bytes 8556548 | tf_op jit(solution)/shard_map/while/body/eval_jaxpr/dot_general | solution.py:111
  178.3 4.0 %fusion.66 = f32[512]{0:T(512)S(1)} fusion(f32[4096,512]{1,0:T(8,128)} %get-tuple-element.839, s32[512]{0:T(512)S(1)} %get-tuple-element.935, s32[4096]{0:T(1024)S(1)} %iota_add_fusion.4), kind=kLoop, calls=%fused_computation.4.clone.clone.1 | loop fusion | flops 6290944 | bytes 8409088 | tf_op jit(solution)/shard_map/while/body/eval_jaxpr/reduce_sum | solution.py:117
  182.4 4.2 %fusion.65 = (f32[512]{0:T(512)S(1)}, f32[4096,512]{1,0:T(8,128)}) fusion(f32[4096]{0:T(1024)S(1)} %multiply_reduce_fusion.4, bf16[16,512]{1,0:T(8,128)(2,1)S(1)} %get-tuple-element.931, bf16[4,16,4096]{2,1,0:T(8,128)(2,1)S(1)} %get-tuple-element.930, s32[]{:T(128)} %get-tuple-element.913, f32[512]{0:T(512)S(1)} %get-tuple-element.929), kind=kOutput, calls=%fused_computation.80.clone.clone.1 | convolution fusion | flops 77594112 | bytes 8556548 | tf_op jit(solution)/shard_map/while/body/eval_jaxpr/dot_general | solution.py:111
  187.8 4.0 %fusion.66 = f32[512]{0:T(512)S(1)} fusion(f32[4096,512]{1,0:T(8,128)} %get-tuple-element.839, s32[512]{0:T(512)S(1)} %get-tuple-element.935, s32[4096]{0:T(1024)S(1)} %iota_add_fusion.4), kind=kLoop, calls=%fused_computation.4.clone.clone.1 | loop fusion | flops 6290944 | bytes 8409088 | tf_op jit(solution)/shard_map/while/body/eval_jaxpr/reduce_sum | solution.py:117
  191.9 4.2 %fusion.65 = (f32[512]{0:T(512)S(1)}, f32[4096,512]{1,0:T(8,128)}) fusion(f32[4096]{0:T(1024)S(1)} %multiply_reduce_fusion.4, bf16[16,512]{1,0:T(8,128)(2,1)S(1)} %get-tuple-element.931, bf16[4,16,4096]{2,1,0:T(8,128)(2,1)S(1)} %get-tuple-element.930, s32[]{:T(128)} %get-tuple-element.913, f32[512]{0:T(512)S(1)} %get-tuple-element.929), kind=kOutput, calls=%fused_computation.80.clone.clone.1 | convolution fusion | flops 77594112 | bytes 8556548 | tf_op jit(solution)/shard_map/while/body/eval_jaxpr/dot_general | solution.py:111
  197.3 4.0 %fusion.66 = f32[512]{0:T(512)S(1)} fusion(f32[4096,512]{1,0:T(8,128)} %get-tuple-element.839, s32[512]{0:T(512)S(1)} %get-tuple-element.935, s32[4096]{0:T(1024)S(1)} %iota_add_fusion.4), kind=kLoop, calls=%fused_computation.4.clone.clone.1 | loop fusion | flops 6290944 | bytes 8409088 | tf_op jit(solution)/shard_map/while/body/eval_jaxpr/reduce_sum | solution.py:117
  201.3 4.2 %fusion.65 = (f32[512]{0:T(512)S(1)}, f32[4096,512]{1,0:T(8,128)}) fusion(f32[4096]{0:T(1024)S(1)} %multiply_reduce_fusion.4, bf16[16,512]{1,0:T(8,128)(2,1)S(1)} %get-tuple-element.931, bf16[4,16,4096]{2,1,0:T(8,128)(2,1)S(1)} %get-tuple-element.930, s32[]{:T(128)} %get-tuple-element.913, f32[512]{0:T(512)S(1)} %get-tuple-element.929), kind=kOutput, calls=%fused_computation.80.clone.clone.1 | convolution fusion | flops 77594112 | bytes 8556548 | tf_op jit(solution)/shard_map/while/body/eval_jaxpr/dot_general | solution.py:111
  206.8 4.0 %fusion.66 = f32[512]{0:T(512)S(1)} fusion(f32[4096,512]{1,0:T(8,128)} %get-tuple-element.839, s32[512]{0:T(512)S(1)} %get-tuple-element.935, s32[4096]{0:T(1024)S(1)} %iota_add_fusion.4), kind=kLoop, calls=%fused_computation.4.clone.clone.1 | loop fusion | flops 6290944 | bytes 8409088 | tf_op jit(solution)/shard_map/while/body/eval_jaxpr/reduce_sum | solution.py:117
  210.8 5.2 %all-gather.2 = f32[4,1,512]{2,1,0:T(1,128)S(1)} all-gather(f32[1,1,512]{2,1,0:T(1,128)S(1)} %bitcast.101), channel_id=2, replica_groups=mesh['groups'=2,'frames'=4,'code'=2,'head'=2] {'code','head'}, dimensions={0}, use_global_device_ids=true | all-gather | bytes 10240 | tf_op jit(solution)/shard_map/all_gather | solution.py:21
  216.0 5.2 %all-gather.3 = f32[4,1,512]{2,1,0:T(1,128)S(1)} all-gather(f32[1,1,512]{2,1,0:T(1,128)S(1)} %bitcast.102), channel_id=3, replica_groups=mesh['groups'=2,'frames'=4,'code'=2,'head'=2] {'code','head'}, dimensions={0}, use_global_device_ids=true | all-gather | bytes 10240 | tf_op jit(solution)/shard_map/all_gather | solution.py:21
  (128 shorter events, 35.5 us)
Async XLA Ops:
  7.2 131.9 %copy-start = (bf16[256,1024]{1,0:T(8,128)(2,1)S(1)}, bf16[256,1024]{1,0:T(8,128)(2,1)}, u32[]{:S(2)}) copy-start(bf16[256,1024]{1,0:T(8,128)(2,1)} %param.20) | copy-start | bytes 1572868
  7.2 36.8 %all-gather.8.cloned.1.call-start = ((), (), s32[]{:S(2)}) async-start(), calls=%async_computation.1 | async-start | bytes 1310720 | tf_op jit(solution)/shard_map/all_gather | solution.py:156
  7.2 10.3 %collective-permute-start = (bf16[64,2,1024]{2,1,0:T(2,128)(2,1)}, bf16[64,2,1024]{2,1,0:T(2,128)(2,1)S(1)}, u32[]{:S(2)}, u32[]{:S(2)}) collective-permute-start(bf16[64,2,1024]{2,1,0:T(2,128)(2,1)} %param.16), channel_id=1, source_target_pairs={{0,4},{4,8},{8,12},{1,5},{5,9},{9,13},{2,6},{6,10},{10,14},{3,7},{... | collective-permute-start | bytes 786440 | tf_op jit(solution)/shard_map/ppermute | solution.py:17
  20.9 4.3 %copy-start.7 = (f32[1024]{0:T(1024)S(1)}, f32[1024]{0:T(1024)}, u32[]{:S(2)}) copy-start(f32[1024]{0:T(1024)} %param.18) | copy-start | bytes 12292
  20.9 5.2 %copy-start.1 = (bf16[1024,3,256]{2,0,1:T(8,128)(2,1)S(1)}, bf16[1024,3,256]{2,0,1:T(8,128)(2,1)}, u32[]{:S(2)}) copy-start(bf16[1024,3,256]{2,0,1:T(8,128)(2,1)} %param.19) | copy-start | bytes 4718596
  25.2 21.5 %copy-start.2 = (bf16[128,1024]{1,0:T(8,128)(2,1)}, bf16[128,1024]{1,0:T(8,128)(2,1)S(1)}, u32[]{:S(2)}) copy-start(bf16[128,1024]{1,0:T(8,128)(2,1)S(1)} %get-tuple-element.618) | copy-start | bytes 786436
  26.1 48.1 %all-gather.10.cloned.1.call-start = ((), (), s32[]{:S(2)}) async-start(), calls=%async_computation.2 | async-start | bytes 1310720 | tf_op jit(solution)/shard_map/all_gather | solution.py:47
  47.6 55.6 %all-gather.12.cloned.1.call-start = ((), (), s32[]{:S(2)}) async-start(), calls=%async_computation.3 | async-start | bytes 1310720 | tf_op jit(solution)/shard_map/all_gather | solution.py:48
  48.3 118.1 %reduce-scatter.2.cloned.1.call-start = ((), (), s32[]{:S(2)}) async-start(), calls=%async_computation.4 | async-start | bytes 1310720 | tf_op jit(solution)/shard_map/reduce_scatter | solution.py:170
  108.9 31.7 %copy-start.8 = (s32[256,2]{0,1:T(2,128)S(1)}, s32[256,2]{0,1:T(2,128)}, u32[]{:S(2)}) copy-start(s32[256,2]{0,1:T(2,128)} %param.23) | copy-start | bytes 6148
  139.0 1.9 copy-start.4
  139.0 27.4 %copy-start.3 = (bf16[128,1024]{1,0:T(8,128)(2,1)S(1)}, bf16[128,1024]{1,0:T(8,128)(2,1)}, u32[]{:S(2)}) copy-start(bf16[128,1024]{1,0:T(8,128)(2,1)} %copy-done.2) | copy-start | bytes 786436
  139.0 28.4 %copy-start.6 = (bf16[1024,16]{0,1:T(8,128)(2,1)S(1)}, bf16[1024,16]{0,1:T(8,128)(2,1)}, u32[]{:S(2)}) copy-start(bf16[1024,16]{0,1:T(8,128)(2,1)} %param.21) | copy-start | bytes 98308
  140.7 32.1 %copy-start.5 = (s32[256,2]{1,0:T(8,128)}, s32[256,2]{1,0:T(8,128)S(1)}, u32[]{:S(2)}) copy-start(s32[256,2]{1,0:T(8,128)S(1)} %copy.36) | copy-start | bytes 6148
Sparse Core Ops, SparseCore 0:
  26.2 17.6 all-gather.7
  47.7 26.4 all-gather.9
  75.8 27.3 all-gather.11
  140.7 25.6 reduce-scatter.1
where the time goes:
time: 233 us; the launch traced here: 230 us
  waiting for transfers between devices  97.5 us (42%)
  matrix products  42 us (18%)
  other arithmetic  26.3 us (11%)
  local copies, waits for them, and re-layouts  24.7 us (11%)
  blocking collectives  15.6 us (7%)
  between operations  14.1 us (6%)
  loops' own time  8.4 us (4%)
    all_gather x1, waiting for transfers between devices, attend_slab(): key_part = lax.all_gather(keys, 'frames', axis=0, tiled=True)  24.8 us
    reduce_scatter x1, waiting for transfers between devices, shards(): lax.psum_scatter(jnp.dot(attended, out_weight, preferred_element_type=jnp...  24.8 us
    all_gather x1, waiting for transfers between devices, attend_slab(): value_part = lax.all_gather(values, 'frames', axis=0, tiled=True)  23.3 us
    dot_general x4, matrix products, scan_visit(): lax.dot_general(latent_t, code_block, (((0,), (0,)), ((), ())), preferred...  16.6 us
    all_gather x1, waiting for transfers between devices, shards(): lax.all_gather(normed, ('code', 'head'), axis=0, tiled=True)  16 us
    reduce_sum x4, other arithmetic, scan_visit(): jnp.sum(jnp.where(labels[None, :] == wanted[:, None], distance, 0.0), axi...  15.9 us
    all_gather x2, blocking collectives, merged(): everything = jax.tree.map(lambda part: lax.all_gather(part, axis), value)  10.4 us
    dot_general x4, matrix products, compute(): jnp.einsum('qhk,khd->qhd', weights.astype(jnp.bfloat16), value_block, pre...  9.25 us
  transfers between devices with their start and end apart: 5, of which 5 were waited for; matrix products, arithmetic and copies ran while one was open for 4% of the time, Pallas kernels for 0%

commit v1 on v0

v1 whole, which is shorter than its diff:
```python
import functools
import math

import jax
import jax.numpy as jnp
from jax import lax
from jax.experimental import pallas as pl
from jax.experimental.pallas import tpu as pltpu
from jax.sharding import PartitionSpec as P

HEADS = 16
EPSILON = 1e-06
LANES = 128
EXT = 32

VMEM = pl.BlockSpec(memory_space=pltpu.VMEM)
SMEM = pl.BlockSpec(memory_space=pltpu.SMEM)


def call(kernel, out_shape, operands, scratch=(), scalars=0, flops=0, moved=0, name=None, limit=20):
    single = not isinstance(out_shape, (tuple, list))
    specs = [SMEM] * scalars + [VMEM] * (len(operands) - scalars)
    return pl.pallas_call(
        kernel,
        out_shape=out_shape,
        in_specs=specs,
        out_specs=VMEM if single else [VMEM] * len(out_shape),
        scratch_shapes=list(scratch),
        compiler_params=pltpu.CompilerParams(vmem_limit_bytes=limit << 20),
        cost_estimate=pl.CostEstimate(flops=flops, bytes_accessed=moved, transcendentals=0),
        name=name,
    )(*operands)


def shifted(block, axis, distance, around):
    size = lax.axis_size(axis)
    if around:
        route = [(i, (i + distance) % size) for i in range(size)]
    else:
        route = [(i, i + distance) for i in range(size) if i + distance < size]
    return lax.ppermute(block, axis, route)


def conv_kernel(count, keep, *refs):
    currents, earliers = refs[:count], refs[count : 2 * count]
    w_ref, gain_ref = refs[2 * count : 2 * count + 2]
    outs = refs[2 * count + 2 : -1]
    block_ref = refs[-1]
    rows, width = currents[0].shape
    half = rows // 2
    taps = [[], [], []]
    for cur, prev in zip(currents, earliers):
        taps[0] += [cur[...]]
        taps[1] += [prev[half:, :], cur[:half, :]]
        taps[2] += [prev[...]]
    taps = [t[0] if len(t) == 1 else jnp.concatenate(t, axis=0) for t in taps]
    chunk = min(width, 256)
    total = jnp.zeros((count * rows, 1), jnp.float32)
    for j in range(0, width, chunk):
        mixed = sum(
            jnp.dot(taps[k], w_ref[k, :, j : j + chunk], preferred_element_type=jnp.float32)
            for k in range(3)
        )
        silu = mixed / (1.0 + jnp.exp(-mixed))
        block = (taps[0][:, j : j + chunk].astype(jnp.float32) + silu).astype(jnp.bfloat16)
        block_ref[:, j : j + chunk] = block
        block32 = block.astype(jnp.float32)
        total = total + jnp.sum(block32 * block32, axis=1, keepdims=True)
    inverse = lax.rsqrt(total / width + EPSILON)
    for i in range(count):
        part = slice(i * rows, (i + 1) * rows)
        block32 = block_ref[part, :].astype(jnp.float32)
        outs[i][...] = (block32 * inverse[part] * gain_ref[...]).astype(jnp.bfloat16)
    if keep:
        outs[count][...] = block_ref[:rows, :]


def conv_norm(pairs, conv_weight, gain, keep, name):
    count = len(pairs)
    rows, width = pairs[0][0].shape
    shape = jax.ShapeDtypeStruct((rows, width), jnp.bfloat16)
    return call(
        functools.partial(conv_kernel, count, keep),
        [shape] * (count + keep),
        [p[0] for p in pairs] + [p[1] for p in pairs] + [conv_weight, gain],
        scratch=[pltpu.VMEM((count * rows, width), jnp.bfloat16)],
        flops=6 * count * rows * width * width,
        moved=conv_weight.size * 2,
        name=name,
        limit=16,
    )


def slab_kernel(ncol, first, last, head_dim, *refs):
    refs = list(refs)
    valid_ref = None if first else refs.pop(0)
    columns = [refs.pop(0) for _ in range(ncol)]
    w_ref = refs.pop(0)
    if first:
        q_old = acc_old = top_old = None
    else:
        q_old, acc_old, top_old = refs.pop(0), refs.pop(0), refs.pop(0)
    if last:
        outs = [refs.pop(0) for _ in range(ncol)]
        if first:
            q_new = None
        acc_new = top_new = None
    else:
        if first:
            q_new = refs.pop(0)
        acc_new, top_new = refs.pop(0), refs.pop(0)
    x_ref = refs.pop(0)
    if last:
        acc_new, top_new = refs.pop(0), refs.pop(0)
        if first:
            q_new = refs.pop(0)

    half = columns[0].shape[0] // 2
    part = ncol * half
    rows = 2 * part
    tiles = w_ref.shape[2] // LANES
    per = LANES // head_dim
    heads = tiles * per
    scale = 1.0 / math.sqrt(head_dim)

    def work():
        for f in range(2):
            for j in range(ncol):
                at = f * part + j * half
                x_ref[at : at + half, :] = columns[j][f * half : (f + 1) * half, :]
        lane = lax.broadcasted_iota(jnp.int32, (1, LANES), 1)
        for t in range(tiles):
            cols = slice(t * LANES, (t + 1) * LANES)
            if first:
                q = jnp.dot(x_ref[...], w_ref[0, :, cols], preferred_element_type=jnp.float32)
                q_new[:, cols] = (q.astype(jnp.bfloat16).astype(jnp.float32) * scale).astype(jnp.bfloat16)
                queries = q_new[:, cols]
            else:
                queries = q_old[:, cols]
            keys = jnp.dot(x_ref[...], w_ref[1, :, cols], preferred_element_type=jnp.float32).astype(jnp.bfloat16)
            values = jnp.dot(x_ref[...], w_ref[2, :, cols], preferred_element_type=jnp.float32).astype(jnp.bfloat16)
            for e in range(per):
                h = t * per + e
                inside = (lane >= e * head_dim) & (lane < (e + 1) * head_dim)
                ones_at = ((e + 1) % per) * head_dim
                filler = jnp.where(lane == ones_at, 1.0, 0.0).astype(jnp.bfloat16)
                head_q = jnp.where(inside, queries, jnp.zeros_like(queries))
                head_v = jnp.where(inside, values, jnp.broadcast_to(filler, values.shape))
                for f in range(2):
                    qs = slice(f * part, (f + 1) * part)
                    depth = (f + 1) * part if first else rows
                    scores = lax.dot_general(
                        head_q[qs], keys[:depth], (((1,), (1,)), ((), ())), preferred_element_type=jnp.float32
                    )
                    top = jnp.max(scores, axis=1, keepdims=True)
                    if not first:
                        before = top_old[qs, h : h + 1]
                        top = jnp.maximum(top, before)
                    weights = jnp.exp(scores - top).astype(jnp.bfloat16)
                    acc = jnp.dot(weights, head_v[:depth], preferred_element_type=jnp.float32)
                    if not first:
                        acc = acc + acc_old[h, qs, :] * jnp.exp(before - top)
                    acc_new[h, qs, :] = acc
                    top_new[qs, h : h + 1] = top

    if first:
        work()
    else:
        valid = valid_ref[0] > 0

        @pl.when(valid)
        def _():
            work()

        @pl.when(jnp.logical_not(valid))
        def _():
            acc_new[...] = acc_old[...]
            top_new[...] = top_old[...]

    if last:
        lane = lax.broadcasted_iota(jnp.int32, (1, LANES), 1)
        for t in range(tiles):
            result = None
            for e in range(per):
                h = t * per + e
                ones_at = ((e + 1) % per) * head_dim
                acc = acc_new[h]
                mine = acc / acc[:, ones_at : ones_at + 1]
                inside = (lane >= e * head_dim) & (lane < (e + 1) * head_dim)
                result = mine if result is None else jnp.where(inside, mine, result)
            result = result.astype(jnp.bfloat16)
            for f in range(2):
                for j in range(ncol):
                    at = f * part + j * half
                    outs[j][f * half : (f + 1) * half, t * LANES : (t + 1) * LANES] = result[at : at + half]


def attend_slab(columns, weights, state, valid, last, head_dim, name):
    ncol = len(columns)
    first = state is None
    crow, width = columns[0].shape
    rows = ncol * crow
    local = weights.shape[2]
    heads = local // head_dim
    q_shape = ((rows, local), jnp.bfloat16)
    acc_shape = ((heads, rows, LANES), jnp.float32)
    top_shape = ((rows, LANES), jnp.float32)
    outs, scratch = [], [pltpu.VMEM((rows, width), jnp.bfloat16)]
    if last:
        outs += [jax.ShapeDtypeStruct((crow, local), jnp.bfloat16)] * ncol
        scratch += [pltpu.VMEM(*acc_shape), pltpu.VMEM(*top_shape)]
        if first:
            scratch += [pltpu.VMEM(*q_shape)]
    else:
        if first:
            outs += [jax.ShapeDtypeStruct(*q_shape)]
        outs += [jax.ShapeDtypeStruct(*acc_shape), jax.ShapeDtypeStruct(*top_shape)]
    operands = ([] if first else [valid]) + list(columns) + [weights] + ([] if first else list(state))
    result = call(
        functools.partial(slab_kernel, ncol, first, last, head_dim),
        outs,
        operands,
        scratch=scratch,
        scalars=0 if first else 1,
        flops=2 * rows * width * 3 * local + 4 * heads * rows * rows * LANES,
        moved=weights.size * 2,
        name=name,
        limit=24,
    )
    if last:
        return result
    return result if first else [state[0]] + list(result)


def codes_kernel(pieces, at_ref, wanted_ref, *refs):
    blocks = refs[:pieces]
    ext_ref, chosen_ref, square_ref = refs[pieces:]
    depth, length = blocks[0].shape
    for i in range(pieces):
        start = pl.multiple_of(at_ref[i], length)
        block = blocks[i][...]
        block32 = block.astype(jnp.float32)
        squares = jnp.sum(block32 * block32, axis=0, keepdims=True)
        high = squares.astype(jnp.bfloat16)
        rest = squares - high.astype(jnp.float32)
        middle = rest.astype(jnp.bfloat16)
        low = (rest - middle.astype(jnp.float32)).astype(jnp.bfloat16)
        row = lax.broadcasted_iota(jnp.int32, (EXT - depth, length), 0)
        spread = lambda v: jnp.broadcast_to(v.astype(jnp.float32), row.shape)
        extra = jnp.where(row == 0, spread(high), jnp.where(row == 1, spread(middle), jnp.where(row == 2, spread(low), 0.0)))
        ext_ref[:depth, pl.ds(start, length)] = block
        ext_ref[depth:, pl.ds(start, length)] = extra.astype(jnp.bfloat16)
    tokens = wanted_ref.shape[0]
    lane = lax.broadcasted_iota(jnp.int32, (depth, LANES), 1)

    def pick(base):
        def one(i, so_far):
            code = wanted_ref[base + i]
            tile = ext_ref[:depth, pl.ds(pl.multiple_of(code // LANES * LANES, LANES), LANES)]
            turned = pltpu.roll(tile.astype(jnp.float32), lax.rem(i - lax.rem(code, LANES) + LANES, LANES), 1)
            return jnp.where(lane == i, turned, so_far)

        return lax.fori_loop(0, min(LANES, tokens - base), one, jnp.zeros((depth, LANES), jnp.float32), unroll=8)

    for base in range(0, tokens, LANES):
        chosen = pick(base)
        chosen_ref[:, base : base + LANES] = chosen
        square_ref[:, base : base + LANES] = jnp.sum(chosen * chosen, axis=0, keepdims=True)


def prepare_codes(pieces, starts, wanted, codes):
    depth = pieces[0].shape[0]
    tokens = -(-wanted.shape[0] // LANES) * LANES
    return call(
        functools.partial(codes_kernel, len(pieces)),
        [
            jax.ShapeDtypeStruct((EXT, codes), jnp.bfloat16),
            jax.ShapeDtypeStruct((depth, tokens), jnp.float32),
            jax.ShapeDtypeStruct((1, tokens), jnp.float32),
        ],
        [starts, wanted] + list(pieces),
        scalars=2,
        flops=codes * EXT * 200,
        moved=codes * EXT * 2,
        name="codes",
        limit=16,
    )


def tail_kernel(ncol, halves, order_ref, *refs):
    refs = list(refs)
    attended = [refs.pop(0) for _ in range(ncol)]
    matrices = [[refs.pop(0) for _ in range(halves[i])] for i in range(ncol)]
    block_ref, latent_w_ref, ext_ref, chosen_ref, square_ref = refs[:5]
    encoded_ref, least_ref, gap_ref = refs[5:8]
    joined = refs[8]
    rows, width = block_ref.shape
    total = jnp.zeros((rows, width), jnp.float32)
    for i in range(ncol):
        if halves[i] == 1:
            total += jnp.dot(attended[i][...], matrices[i][0][...], preferred_element_type=jnp.float32)
        else:
            size = matrices[i][0].shape[0]
            for k in range(halves[i]):
                joined[pl.ds(pl.multiple_of(order_ref[k] * size, size), size), :] = matrices[i][k][...]
            total += jnp.dot(attended[i][...], joined[...], preferred_element_type=jnp.float32)
    encoded = (block_ref[...].astype(jnp.float32) + total).astype(jnp.bfloat16)
    encoded_ref[...] = encoded
    depth = latent_w_ref.shape[0]
    latent_t = lax.dot_general(
        latent_w_ref[...], encoded, (((1,), (1,)), ((), ())), preferred_element_type=jnp.float32
    ).astype(jnp.bfloat16).astype(jnp.float32)
    own = jnp.sum(latent_t * latent_t, axis=0, keepdims=True)
    row = lax.broadcasted_iota(jnp.int32, (EXT - depth, rows), 0)
    full = jnp.concatenate([latent_t * -2.0, jnp.where(row < 3, 1.0, 0.0)], axis=0)
    left = full.T.astype(jnp.bfloat16)
    codes = ext_ref.shape[1]
    chunk = math.gcd(codes, 2048)

    def visit(i, least):
        dots = jnp.dot(left, ext_ref[:, pl.ds(pl.multiple_of(i * chunk, chunk), chunk)], preferred_element_type=jnp.float32)
        parts = [dots[:, c : c + LANES] for c in range(0, chunk, LANES)]
        while len(parts) > 1:
            parts = [jnp.minimum(a, b) for a, b in zip(parts[::2], parts[1::2])]
        return jnp.minimum(least, parts[0])

    least = lax.fori_loop(0, codes // chunk, visit, jnp.full((rows, LANES), 3e38, jnp.float32))
    least = jnp.min(least.T, axis=0, keepdims=True)
    nearest = (own + least) / depth
    cross = jnp.sum(latent_t * chosen_ref[:, :rows], axis=0, keepdims=True)
    reference = (own - 2.0 * cross + square_ref[:, :rows]) / depth
    least_ref[...] = nearest
    gap_ref[...] = reference - nearest


def shards(video, conv_weight, norm_gain, qkv_weight, out_weight, latent_weight, codebook, reference_codes):
    positions, frames_here, width = video.shape
    slabs, across, cores = (lax.axis_size(a) for a in ("frames", "code", "head"))
    sides = lax.axis_size("groups")
    slab, column, core, side = (lax.axis_index(a) for a in ("frames", "code", "head", "groups"))
    head_dim = width // HEADS
    rows = positions * frames_here

    own = jnp.transpose(video, (1, 0, 2)).reshape(rows, width)
    projection = jnp.transpose(qkv_weight, (1, 0, 2))
    gain = norm_gain.reshape(1, width)

    raw = [own]
    for d in range(1, slabs):
        raw.append(shifted(raw[-1], "frames", 1, False))
    raw.append(jnp.zeros_like(own))

    def shard_halves(array, axis):
        share = array.shape[axis] // sides
        mine = lax.dynamic_slice_in_dim(array, side * share, share, axis)
        pieces = []
        for dx in range(across):
            if dx == 0:
                got = [array]
            else:
                first = shifted(mine, "code", dx, True)
                got = [first] + [shifted(first, "groups", dy, True) for dy in range(1, sides)]
            pieces.append(got)
        result = []
        for dx in range(across):
            for dc in range(cores):
                result.append([g if dc == 0 else shifted(g, "head", dc, True) for g in pieces[dx]])
        return result

    matrices = shard_halves(out_weight, 0)
    code_pieces = shard_halves(codebook, 1)
    order = jnp.stack([lax.rem(side - dy + sides, sides) for dy in range(sides)]).astype(jnp.int32)
    shard_codes = codebook.shape[1]
    starts, flat = [], []
    for dx in range(across):
        for dc in range(cores):
            base = (lax.rem(column - dx + across, across) * cores + lax.rem(core - dc + cores, cores)) * shard_codes
            got = code_pieces[dx * cores + dc]
            if len(got) == 1:
                share = shard_codes // sides
                for y in range(sides):
                    flat.append(got[0][:, y * share : (y + 1) * share])
                    starts.append(base + y * share)
            else:
                for dy, piece in enumerate(got):
                    flat.append(piece)
                    starts.append(base + lax.rem(side - dy + sides, sides) * (shard_codes // sides))
    mine = lax.dynamic_slice_in_dim(reference_codes, (column * cores + core) * positions, positions, 0)
    wanted = jnp.transpose(mine).reshape(rows)
    extended, chosen, chosen_square = prepare_codes(
        flat, jnp.stack(starts).astype(jnp.int32), wanted, shard_codes * across * cores
    )

    def spread(columns):
        return [c if dc == 0 else shifted(c, "head", dc, True) for c in columns for dc in range(cores)]

    def exchanged(normed):
        return [shifted(normed, "code", dx, True) for dx in range(1, across)]

    state, outs, first_others = None, None, None
    for d in range(slabs):
        keep = d == 0
        result = conv_norm([(raw[d], raw[d + 1])], conv_weight, gain, keep, f"conv{d}")
        normed = result[0]
        if keep:
            block_input = result[1]
        if d == 0:
            others = first_others = exchanged(normed)
        elif d < slabs - 1:
            others = exchanged(normed)
        else:
            others = [lax.ppermute(o, "frames", [(0, slabs - 1)]) for o in first_others]
        valid = (slab >= d).astype(jnp.int32).reshape(1)
        state = attend_slab(
            spread([normed] + others), projection, state, valid, d == slabs - 1, head_dim, f"slab{d}"
        )
    outs = state

    returned = []
    for dx in range(across):
        for dc in range(cores):
            piece = outs[dx * cores + dc]
            if dc:
                piece = shifted(piece, "head", -dc, True)
            if dx:
                piece = shifted(piece, "code", -dx, True)
            returned.append(piece)
    def opposite(i):
        dx, dc = divmod(i, cores)
        return (-dx % across) * cores + (-dc % cores)

    meeting = [matrices[opposite(i)] for i in range(across * cores)]
    halves = [len(m) for m in meeting]
    encoded, least, gap = call(
        functools.partial(tail_kernel, across * cores, halves),
        [
            jax.ShapeDtypeStruct((rows, width), jnp.bfloat16),
            jax.ShapeDtypeStruct((1, rows), jnp.float32),
            jax.ShapeDtypeStruct((1, rows), jnp.float32),
        ],
        [order] + returned + [m for ms in meeting for m in ms]
        + [block_input, jnp.transpose(latent_weight), extended, chosen, chosen_square],
        scratch=[pltpu.VMEM(out_weight.shape, jnp.bfloat16)],
        scalars=1,
        flops=2 * rows * width * width + rows * extended.shape[1] * 128,
        moved=extended.size * 2 + width * width * 2,
        name="tail",
        limit=24,
    )
    split = lambda v: jnp.transpose(v.reshape(frames_here, positions))
    return (
        jnp.transpose(encoded.reshape(frames_here, positions, width), (1, 0, 2)),
        split(least),
        split(gap),
    )


def solution(mesh):
    return jax.shard_map(
        shards,
        mesh=mesh,
        in_specs=(
            P(("code", "head"), ("groups", "frames"), None),
            P(),
            P(),
            P(None, None, ("code", "head")),
            P(("code", "head"), None),
            P(),
            P(None, ("code", "head")),
            P(None, ("groups", "frames")),
        ),
        out_specs=(
            P(("code", "head"), ("groups", "frames"), None),
            P(("code", "head"), ("groups", "frames")),
            P(("code", "head"), ("groups", "frames")),
        ),
        check_vma=False,
    )
```

time: 233 us -> 103 us (0.44)
  waiting for transfers between devices: 97.5 us -> 19.6 us
  Pallas kernels: 0 us -> 44.7 us
  matrix products: 42 us -> 0 us
  other arithmetic: 26.3 us -> 1.4 us
  starting transfers between devices: 1.76 us -> 18.7 us
  blocking collectives: 15.6 us -> 0 us
  between operations: 14.1 us -> 0.98 us
  loops' own time: 8.4 us -> 0 us
  local copies, waits for them, and re-layouts: 24.7 us -> 17.2 us
    all_gather x3 -> x0, waiting for transfers between devices: 64.2 us -> none  [the longest x1 24.8 us: attend_slab(): key_part = lax.all_gather(keys, 'frames', axis=0, tiled=True)]
    pallas_call x0 -> x10, Pallas kernels: none -> 44.7 us  [call(): pl.pallas_call(kernel, out_shape=out_shape, in_specs=specs, out_specs=VME...]
    dot_general x16 -> x0, matrix products: 42 us -> none  [the longest x4 16.6 us: scan_visit(): lax.dot_general(latent_t, code_block, (((0,), (0,)), ((), ())), preferred...]
    reduce_scatter x1 -> x0, waiting for transfers between devices: 24.8 us -> none  [shards(): lax.psum_scatter(jnp.dot(attended, out_weight, preferred_element_type=jnp...]
    reduce_sum x13 -> x0, other arithmetic: 20.3 us -> none  [the longest x4 15.9 us: scan_visit(): jnp.sum(jnp.where(labels[None, :] == wanted[:, None], distance, 0.0), axi...]
    ppermute x1 -> x29, starting transfers between devices: 1.42 us -> 18.7 us  [the longest x28 17.4 us: shifted(): return lax.ppermute(block, axis, route)]
    all_gather x3 -> x0, blocking collectives: 15.6 us -> none  [the longest x2 10.4 us: merged(): everything = jax.tree.map(lambda part: lax.all_gather(part, axis), value)]
    ppermute x1 -> x29, waiting for transfers between devices: 7.82 us -> 19.6 us  [the longest x28 19.6 us: shifted(): return lax.ppermute(block, axis, route)]
  transfers between devices with their start and end apart: 5 -> 29, of which waited for: 5 -> 4; matrix products, arithmetic and copies ran while one was open for 4% -> 2% of each run, Pallas kernels for 0% -> 34%
where the time goes in v1:
time: 103 us
  Pallas kernels  44.7 us (43%)
  waiting for transfers between devices  19.6 us (19%)
  starting transfers between devices  18.7 us (18%)
  local copies, waits for them, and re-layouts  17.2 us (17%)
  other arithmetic  1.4 us (1%)
    pallas_call x10, Pallas kernels, call(): pl.pallas_call(kernel, out_shape=out_shape, in_specs=specs, out_specs=VME...  44.7 us
    ppermute x28, waiting for transfers between devices, shifted(): return lax.ppermute(block, axis, route)  19.6 us
    ppermute x28, starting transfers between devices, shifted(): return lax.ppermute(block, axis, route)  17.4 us
    unnamed x36, local copies, waits for them, and re-layouts  11.9 us
  transfers between devices with their start and end apart: 29, of which 4 were waited for; matrix products, arithmetic and copies ran while one was open for 2% of the time, Pallas kernels for 34%

profile of v1, /device:TPU:24, one launch (start us, length us, event | category | flops | bytes accessed | tf_op | source)
XLA Modules:
  0.0 102.6 jit_solution(17625329868326026034)
XLA Ops:
  0.6 1.0 copy.11
  1.7 1.3 %collective-permute-start = (bf16[128,1024]{1,0:T(8,128)(2,1)S(1)}, bf16[128,1024]{1,0:T(8,128)(2,1)S(1)}, u32[]{:S(2)}, u32[]{:S(2)}) collective-permute-start(bf16[128,1024]{1,0:T(8,128)(2,1)S(1)} %bitcast.26), channel_id=1, source_target_pairs={{0,4},{4,8},{8,12},{1,5},{5,9},{9,13},{2,6},{6,10},{10,14},{3,7},{... | collective-permute-start | bytes 786440 | tf_op jit(solution)/shard_map/ppermute | solution.py:41
  3.0 8.6 %collective-permute-done.refs_1_.refs_0_ = bf16[128,1024]{1,0:T(8,128)(2,1)S(1)} collective-permute-done((bf16[128,1024]{1,0:T(8,128)(2,1)S(1)}, bf16[128,1024]{1,0:T(8,128)(2,1)S(1)}, u32[]{:S(2)}, u32[]{:S(2)}) %collective-permute-start) | collective-permute-done | bytes 262176 | tf_op jit(solution)/shard_map/ppermute | solution.py:41
  11.6 1.3 %collective-permute-start.1 = (bf16[128,1024]{1,0:T(8,128)(2,1)S(1)}, bf16[128,1024]{1,0:T(8,128)(2,1)S(1)}, u32[]{:S(2)}, u32[]{:S(2)}) collective-permute-start(bf16[128,1024]{1,0:T(8,128)(2,1)S(1)} %collective-permute-done.refs_1_.refs_0_), channel_id=1, source_target_pairs={{0,4},{4,8},{8,12},{1,5},{5,9},{9,13},{2,6},{6,10},{10,14},{3,7},{... | collective-permute-start | bytes 786440 | tf_op jit(solution)/shard_map/ppermute | solution.py:41
  12.9 1.3 %constant_dynamic-slice_fusion = (bf16[16,8192]{1,0:T(8,128)(2,1)S(1)}, bf16[16,8192]{1,0:T(8,128)(2,1)S(1)}, bf16[16,8192]{1,0:T(8,128)(2,1)S(1)}) fusion(bf16[16,16384]{1,0:T(8,128)(2,1)} %param.14, s32[]{:T(128)S(6)} %select_n.11), kind=kLoop, calls=%fused_computation.2 | loop fusion | bytes 1572868 | tf_op jit(solution)/shard_map/dynamic_slice | solution.py:355
  14.1 1.6 %collective-permute-start.25 = (bf16[16,8192]{1,0:T(8,128)(2,1)S(1)}, bf16[16,8192]{1,0:T(8,128)(2,1)S(1)}, u32[]{:S(2)}, u32[]{:S(2)}) collective-permute-start(bf16[16,8192]{1,0:T(8,128)(2,1)S(1)} %get-tuple-element.41), channel_id=1, source_target_pairs={{0,2},{2,0},{1,3},{3,1},{4,6},{6,4},{5,7},{7,5},{8,10},{10,8},{9,1... | collective-permute-start | bytes 786440 | tf_op jit(solution)/shard_map/ppermute | solution.py:41
  15.7 2.8 %copy-done.1 = bf16[3,1024,1024]{2,1,0:T(8,128)(2,1)S(1)} copy-done((bf16[3,1024,1024]{2,1,0:T(8,128)(2,1)S(1)}, bf16[3,1024,1024]{2,1,0:T(8,128)(2,1)}, u32[]{:S(2)}) %copy-start.1) | copy-done | bytes 6291480
  19.2 2.0 %conv0.1 = (bf16[128,1024]{1,0:T(8,128)(2,1)}, bf16[128,1024]{1,0:T(8,128)(2,1)S(1)}) custom-call(bf16[128,1024]{1,0:T(8,128)(2,1)S(1)} %bitcast.27, bf16[128,1024]{1,0:T(8,128)(2,1)S(1)} %collective-permute-done.refs_1_.refs_0_, bf16[3,1024,1024]{2,1,0:T(8,128)(2,1)S(1)} %copy-done.1, f32[1,1024]{1,0:T(1,128)S(1)} %bitcast.29), custom_call_target="tpu_custom_call" | custom-call | flops 805306368 | bytes 6291456 | tf_op jit(solution)/shard_map/conv0/pallas_call | solution.py:23
  21.7 1.3 %collective-permute-start.2 = (bf16[128,1024]{1,0:T(8,128)(2,1)S(1)}, bf16[128,1024]{1,0:T(8,128)(2,1)S(1)}, u32[]{:S(2)}, u32[]{:S(2)}) collective-permute-start(bf16[128,1024]{1,0:T(8,128)(2,1)S(1)} %collective-permute-done.1.refs_0_.refs_1_), channel_id=1, source_target_pairs={{0,4},{4,8},{8,12},{1,5},{5,9},{9,13},{2,6},{6,10},{10,14},{3,7},{... | collective-permute-start | bytes 786440 | tf_op jit(solution)/shard_map/ppermute | solution.py:41
  23.0 1.6 %collective-permute-start.20 = (bf16[128,1024]{1,0:T(8,128)(2,1)S(1)}, bf16[128,1024]{1,0:T(8,128)(2,1)S(1)}, u32[]{:S(2)}, u32[]{:S(2)}) collective-permute-start(bf16[128,1024]{1,0:T(8,128)(2,1)S(1)} %constant_dynamic-slice_fusion.1), channel_id=1, source_target_pairs={{0,2},{2,0},{1,3},{3,1},{4,6},{6,4},{5,7},{7,5},{8,10},{10,8},{9,1... | collective-permute-start | bytes 786440 | tf_op jit(solution)/shard_map/ppermute | solution.py:41
  24.6 1.5 %collective-permute-start.26 = (bf16[16,8192]{1,0:T(8,128)(2,1)S(1)}, bf16[16,8192]{1,0:T(8,128)(2,1)S(1)}, u32[]{:S(2)}, u32[]{:S(2)}) collective-permute-start(bf16[16,8192]{1,0:T(8,128)(2,1)S(1)} %collective-permute-done.25.refs_4_), channel_id=1, source_target_pairs={{0,16},{16,0},{1,17},{17,1},{2,18},{18,2},{3,19},{19,3},{4,20},{20... | collective-permute-start | bytes 786440 | tf_op jit(solution)/shard_map/ppermute | solution.py:41
  26.1 4.5 %collective-permute-done.4.refs_2_ = bf16[128,1024]{1,0:T(8,128)(2,1)} collective-permute-done((bf16[128,1024]{1,0:T(8,128)(2,1)}, bf16[128,1024]{1,0:T(8,128)(2,1)}, u32[]{:S(2)}, u32[]{:S(2)}) %collective-permute-start.4) | collective-permute-done | bytes 262176 | tf_op jit(solution)/shard_map/ppermute | solution.py:41
  30.6 1.3 %collective-permute-start.5 = (bf16[128,1024]{1,0:T(8,128)(2,1)}, bf16[128,1024]{1,0:T(8,128)(2,1)S(1)}, u32[]{:S(2)}, u32[]{:S(2)}) collective-permute-start(bf16[128,1024]{1,0:T(8,128)(2,1)} %collective-permute-done.4.refs_2_), channel_id=1, source_target_pairs={{0,12},{1,13},{2,14},{3,15},{16,28},{17,29},{18,30},{19,31}} | collective-permute-start | bytes 786440 | tf_op jit(solution)/shard_map/ppermute | solution.py:412
  32.0 2.8 %copy-done.2 = bf16[3,1024,1024]{2,1,0:T(8,128)(2,1)S(1)} copy-done((bf16[3,1024,1024]{2,1,0:T(8,128)(2,1)S(1)}, bf16[3,1024,1024]{2,1,0:T(8,128)(2,1)}, u32[]{:S(2)}) %copy-start.2) | copy-done | bytes 6291480
  34.7 1.3 %conv1.1.refs_1_ = bf16[128,1024]{1,0:T(8,128)(2,1)S(1)} custom-call(bf16[128,1024]{1,0:T(8,128)(2,1)S(1)} %collective-permute-done.refs_1_.refs_0_, bf16[128,1024]{1,0:T(8,128)(2,1)S(1)} %collective-permute-done.1.refs_0_.refs_1_, bf16[3,1024,1024]{2,1,0:T(8,128)(2,1)S(1)} %copy-done.2, f32[1,1024]{1,0:T(1,128)S(1)} %bitcast.30), custom_call_target="tpu_custom_call" | custom-call | flops 805306368 | bytes 6291456 | tf_op jit(solution)/shard_map/conv1/pallas_call | solution.py:23
  36.6 0.9 copy-done.3
  37.5 1.3 %conv2.1.refs_1_ = bf16[128,1024]{1,0:T(8,128)(2,1)S(1)} custom-call(bf16[128,1024]{1,0:T(8,128)(2,1)S(1)} %collective-permute-done.1.refs_0_.refs_1_, bf16[128,1024]{1,0:T(8,128)(2,1)S(1)} %collective-permute-done.2.refs_0_.refs_1_, bf16[3,1024,1024]{2,1,0:T(8,128)(2,1)S(1)} %copy-done.3, f32[1,1024]{1,0:T(1,128)S(1)} %bitcast.31), custom_call_target="tpu_custom_call" | custom-call | flops 805306368 | bytes 6291456 | tf_op jit(solution)/shard_map/conv2/pallas_call | solution.py:23
  38.8 1.3 %conv3.1.refs_1_ = bf16[128,1024]{1,0:T(8,128)(2,1)S(1)} custom-call(bf16[128,1024]{1,0:T(8,128)(2,1)S(1)} %collective-permute-done.2.refs_0_.refs_1_, bf16[128,1024]{1,0:T(8,128)(2,1)S(1)} %broadcast_in_dim.3.refs_1_, bf16[3,1024,1024]{2,1,0:T(8,128)(2,1)S(1)} %copy-done.3, f32[1,1024]{1,0:T(1,128)S(1)} %bitcast.32), custom_call_target="tpu_custom_call" | custom-call | flops 805306368 | bytes 6291456 | tf_op jit(solution)/shard_map/conv3/pallas_call | solution.py:23
  42.6 0.7 copy-done.16
  44.3 5.9 %collective-permute-done.10.refs_3_ = bf16[128,1024]{1,0:T(8,128)(2,1)} collective-permute-done((bf16[128,1024]{1,0:T(8,128)(2,1)S(1)}, bf16[128,1024]{1,0:T(8,128)(2,1)}, u32[]{:S(2)}, u32[]{:S(2)}) %collective-permute-start.10) | collective-permute-done | bytes 262176 | tf_op jit(solution)/shard_map/ppermute | solution.py:41
  51.1 1.4 %copy-done.10 = bf16[1024,3,256]{2,0,1:T(8,128)(2,1)S(1)} copy-done((bf16[1024,3,256]{2,0,1:T(8,128)(2,1)S(1)}, bf16[1024,3,256]{2,0,1:T(8,128)(2,1)}, u32[]{:S(2)}) %copy-start.10) | copy-done | bytes 1572888
  52.5 0.9 copy-done.15
  53.4 0.9 copy-done.17
  54.4 5.8 %slab0.1 = (bf16[512,256]{1,0:T(8,128)(2,1)S(1)}, f32[4,512,128]{2,1,0:T(8,128)S(1)}, f32[512,128]{1,0:T(8,128)S(1)}) custom-call(bf16[128,1024]{1,0:T(8,128)(2,1)} %get-tuple-element.22.refs_0_, bf16[128,1024]{1,0:T(8,128)(2,1)S(1)} %copy-done.15, bf16[128,1024]{1,0:T(8,128)(2,1)} %collective-permute-done.4.refs_2_, bf16[128,1024]{1,0:T(8,128)(2,1)S(1)} %copy-done.17, ...), custom_call_target="tpu_custom_call" | custom-call | flops 1342177280 | bytes 1572864 | tf_op jit(solution)/shard_map/slab0/pallas_call | solution.py:23
  60.2 6.1 %slab1.1 = (f32[4,512,128]{2,1,0:T(8,128)S(1)}, f32[512,128]{1,0:T(8,128)S(1)}) custom-call(s32[1]{0:T(128)} %bitcast.8.refs_0_, bf16[128,1024]{1,0:T(8,128)(2,1)S(1)} %conv1.1.refs_1_, bf16[128,1024]{1,0:T(8,128)(2,1)} %collective-permute-done.12.refs_2_, bf16[128,1024]{1,0:T(8,128)(2,1)} %collective-permute-done.13.refs_3_, ...), custom_call_target="tpu_custom_call" | custom-call | flops 1342177280 | bytes 1572864 | tf_op jit(solution)/shard_map/slab1/pallas_call | solution.py:23
  66.5 1.6 %collective-permute-start.21 = (bf16[128,1024]{1,0:T(8,128)(2,1)S(1)}, bf16[128,1024]{1,0:T(8,128)(2,1)S(1)}, u32[]{:S(2)}, u32[]{:S(2)}) collective-permute-start(bf16[128,1024]{1,0:T(8,128)(2,1)S(1)} %collective-permute-done.20.refs_6_), channel_id=1, source_target_pairs={{0,16},{16,0},{1,17},{17,1},{2,18},{18,2},{3,19},{19,3},{4,20},{20... | collective-permute-start | bytes 786440 | tf_op jit(solution)/shard_map/ppermute | solution.py:41
  68.2 6.1 %slab2.1 = (f32[4,512,128]{2,1,0:T(8,128)S(1)}, f32[512,128]{1,0:T(8,128)S(1)}) custom-call(s32[1]{0:T(128)} %bitcast.7.refs_0_, bf16[128,1024]{1,0:T(8,128)(2,1)S(1)} %conv2.1.refs_1_, bf16[128,1024]{1,0:T(8,128)(2,1)} %collective-permute-done.9.refs_2_, bf16[128,1024]{1,0:T(8,128)(2,1)} %collective-permute-done.10.refs_3_, ...), custom_call_target="tpu_custom_call" | custom-call | flops 1342177280 | bytes 1572864 | tf_op jit(solution)/shard_map/slab2/pallas_call | solution.py:23
  74.4 6.5 %slab3.1 = (bf16[128,256]{1,0:T(8,128)(2,1)S(1)}, bf16[128,256]{1,0:T(8,128)(2,1)S(1)}, bf16[128,256]{1,0:T(8,128)(2,1)S(1)}, bf16[128,256]{1,0:T(8,128)(2,1)S(1)}) custom-call(s32[1]{0:T(128)} %bitcast.2.refs_0_, bf16[128,1024]{1,0:T(8,128)(2,1)S(1)} %conv3.1.refs_1_, bf16[128,1024]{1,0:T(8,128)(2,1)S(1)} %collective-permute-done.3.refs_2_, ...), custom_call_target="tpu_custom_call" | custom-call | flops 1342177280 | bytes 1572864 | tf_op jit(solution)/shard_map/slab3/pallas_call | solution.py:23
  82.6 1.5 %collective-permute-start.18 = (bf16[128,256]{1,0:T(8,128)(2,1)S(1)}, bf16[128,256]{1,0:T(8,128)(2,1)S(1)}, u32[]{:S(2)}, u32[]{:S(2)}) collective-permute-start(bf16[128,256]{1,0:T(8,128)(2,1)S(1)} %collective-permute-done.17), channel_id=1, source_target_pairs={{0,2},{2,0},{1,3},{3,1},{4,6},{6,4},{5,7},{7,5},{8,10},{10,8},{9,1... | collective-permute-start | bytes 196616 | tf_op jit(solution)/shard_map/ppermute | solution.py:41
  84.1 4.0 %codes.1 = (bf16[32,65536]{1,0:T(8,128)(2,1)S(1)}, f32[16,128]{1,0:T(8,128)S(1)}, f32[1,128]{1,0:T(1,128)S(1)}) custom-call(s32[8]{0:T(128)S(1)} %stack.47.at_ref, s32[128]{0:T(128)S(1)} %reshape.47.wanted_ref, bf16[16,8192]{1,0:T(8,128)(2,1)S(1)} %get-tuple-element.43.refs_0_, bf16[16,8192]{1,0:T(8,128)(2,1)S(1)} %get-tuple-element.42.refs_1_, ...), custom_call_target="tpu_custom_call" | custom-call | flops 419430400 | bytes 4194304 | tf_op jit(solution)/shard_map/codes/pallas_call | solution.py:23
  88.2 10.3 %tail.1 = (bf16[128,1024]{1,0:T(8,128)(2,1)S(1)}, f32[1,128]{1,0:T(1,128)S(1)}, f32[1,128]{1,0:T(1,128)S(1)}) custom-call(s32[2]{0:T(128)S(1)} %pad_add_fusion.order_ref, bf16[128,256]{1,0:T(8,128)(2,1)S(1)} %get-tuple-element.30.refs_0_, bf16[128,256]{1,0:T(8,128)(2,1)S(1)} %collective-permute-done.15.refs_1_, ...), custom_call_target="tpu_custom_call" | custom-call | flops 1342177280 | bytes 6291456 | tf_op jit(solution)/shard_map/tail/pallas_call | solution.py:23
  98.5 1.0 copy.14
  (87 shorter events, 11.4 us)
Async XLA Ops:
  0.6 49.6 %copy-start = (s32[256,2]{0,1:T(2,128)S(1)}, s32[256,2]{0,1:T(2,128)}, u32[]{:S(2)}) copy-start(s32[256,2]{0,1:T(2,128)} %param.15) | copy-start | bytes 6148
  1.7 9.9 %collective-permute-start = (bf16[128,1024]{1,0:T(8,128)(2,1)S(1)}, bf16[128,1024]{1,0:T(8,128)(2,1)S(1)}, u32[]{:S(2)}, u32[]{:S(2)}) collective-permute-start(bf16[128,1024]{1,0:T(8,128)(2,1)S(1)} %bitcast.26), channel_id=1, source_target_pairs={{0,4},{4,8},{8,12},{1,5},{5,9},{9,13},{2,6},{6,10},{10,14},{3,7},{... | collective-permute-start | bytes 786440 | tf_op jit(solution)/shard_map/ppermute | solution.py:41
  3.0 20.0 %copy-start.4 = (bf16[256,1024]{1,0:T(8,128)(2,1)S(1)}, bf16[256,1024]{1,0:T(8,128)(2,1)}, u32[]{:S(2)}) copy-start(bf16[256,1024]{1,0:T(8,128)(2,1)} %refs_4_.1) | copy-start | bytes 1572868
  3.0 29.0 %copy-start.8 = (f32[1024]{0:T(1024)S(1)}, f32[1024]{0:T(1024)}, u32[]{:S(2)}) copy-start(f32[1024]{0:T(1024)} %param.10) | copy-start | bytes 12292
  11.6 10.1 %collective-permute-start.1 = (bf16[128,1024]{1,0:T(8,128)(2,1)S(1)}, bf16[128,1024]{1,0:T(8,128)(2,1)S(1)}, u32[]{:S(2)}, u32[]{:S(2)}) collective-permute-start(bf16[128,1024]{1,0:T(8,128)(2,1)S(1)} %collective-permute-done.refs_1_.refs_0_), channel_id=1, source_target_pairs={{0,4},{4,8},{8,12},{1,5},{5,9},{9,13},{2,6},{6,10},{10,14},{3,7},{... | collective-permute-start | bytes 786440 | tf_op jit(solution)/shard_map/ppermute | solution.py:41
  14.1 10.4 %collective-permute-start.25 = (bf16[16,8192]{1,0:T(8,128)(2,1)S(1)}, bf16[16,8192]{1,0:T(8,128)(2,1)S(1)}, u32[]{:S(2)}, u32[]{:S(2)}) collective-permute-start(bf16[16,8192]{1,0:T(8,128)(2,1)S(1)} %get-tuple-element.41), channel_id=1, source_target_pairs={{0,2},{2,0},{1,3},{3,1},{4,6},{6,4},{5,7},{7,5},{8,10},{10,8},{9,1... | collective-permute-start | bytes 786440 | tf_op jit(solution)/shard_map/ppermute | solution.py:41
  21.2 9.5 %collective-permute-start.4 = (bf16[128,1024]{1,0:T(8,128)(2,1)}, bf16[128,1024]{1,0:T(8,128)(2,1)}, u32[]{:S(2)}, u32[]{:S(2)}) collective-permute-start(bf16[128,1024]{1,0:T(8,128)(2,1)} %get-tuple-element.22.refs_0_), channel_id=1, source_target_pairs={{0,2},{2,0},{1,3},{3,1},{4,6},{6,4},{5,7},{7,5},{8,10},{10,8},{9,1... | collective-permute-start | bytes 786440 | tf_op jit(solution)/shard_map/ppermute | solution.py:41
  21.7 14.3 %collective-permute-start.2 = (bf16[128,1024]{1,0:T(8,128)(2,1)S(1)}, bf16[128,1024]{1,0:T(8,128)(2,1)S(1)}, u32[]{:S(2)}, u32[]{:S(2)}) collective-permute-start(bf16[128,1024]{1,0:T(8,128)(2,1)S(1)} %collective-permute-done.1.refs_0_.refs_1_), channel_id=1, source_target_pairs={{0,4},{4,8},{8,12},{1,5},{5,9},{9,13},{2,6},{6,10},{10,14},{3,7},{... | collective-permute-start | bytes 786440 | tf_op jit(solution)/shard_map/ppermute | solution.py:41
  23.0 17.1 %collective-permute-start.20 = (bf16[128,1024]{1,0:T(8,128)(2,1)S(1)}, bf16[128,1024]{1,0:T(8,128)(2,1)S(1)}, u32[]{:S(2)}, u32[]{:S(2)}) collective-permute-start(bf16[128,1024]{1,0:T(8,128)(2,1)S(1)} %constant_dynamic-slice_fusion.1), channel_id=1, source_target_pairs={{0,2},{2,0},{1,3},{3,1},{4,6},{6,4},{5,7},{7,5},{8,10},{10,8},{9,1... | collective-permute-start | bytes 786440 | tf_op jit(solution)/shard_map/ppermute | solution.py:41
  24.6 15.6 %collective-permute-start.7 = (bf16[128,1024]{1,0:T(8,128)(2,1)}, bf16[128,1024]{1,0:T(8,128)(2,1)S(1)}, u32[]{:S(2)}, u32[]{:S(2)}) collective-permute-start(bf16[128,1024]{1,0:T(8,128)(2,1)} %get-tuple-element.22.refs_0_), channel_id=1, source_target_pairs={{0,1},{1,0},{2,3},{3,2},{4,5},{5,4},{6,7},{7,6},{8,9},{9,8},{10,11... | collective-permute-start | bytes 786440 | tf_op jit(solution)/shard_map/ppermute | solution.py:41
  24.6 16.8 %collective-permute-start.26 = (bf16[16,8192]{1,0:T(8,128)(2,1)S(1)}, bf16[16,8192]{1,0:T(8,128)(2,1)S(1)}, u32[]{:S(2)}, u32[]{:S(2)}) collective-permute-start(bf16[16,8192]{1,0:T(8,128)(2,1)S(1)} %collective-permute-done.25.refs_4_), channel_id=1, source_target_pairs={{0,16},{16,0},{1,17},{17,1},{2,18},{18,2},{3,19},{19,3},{4,20},{20... | collective-permute-start | bytes 786440 | tf_op jit(solution)/shard_map/ppermute | solution.py:41
  30.6 10.9 %collective-permute-start.5 = (bf16[128,1024]{1,0:T(8,128)(2,1)}, bf16[128,1024]{1,0:T(8,128)(2,1)S(1)}, u32[]{:S(2)}, u32[]{:S(2)}) collective-permute-start(bf16[128,1024]{1,0:T(8,128)(2,1)} %collective-permute-done.4.refs_2_), channel_id=1, source_target_pairs={{0,12},{1,13},{2,14},{3,15},{16,28},{17,29},{18,30},{19,31}} | collective-permute-start | bytes 786440 | tf_op jit(solution)/shard_map/ppermute | solution.py:412
  36.0 6.5 %collective-permute-start.13 = (bf16[128,1024]{1,0:T(8,128)(2,1)S(1)}, bf16[128,1024]{1,0:T(8,128)(2,1)}, u32[]{:S(2)}, u32[]{:S(2)}) collective-permute-start(bf16[128,1024]{1,0:T(8,128)(2,1)S(1)} %conv1.1.refs_1_), channel_id=1, source_target_pairs={{0,2},{2,0},{1,3},{3,1},{4,6},{6,4},{5,7},{7,5},{8,10},{10,8},{9,1... | collective-permute-start | bytes 786440 | tf_op jit(solution)/shard_map/ppermute | solution.py:41
  40.1 2.5 %collective-permute-start.8 = (bf16[128,1024]{1,0:T(8,128)(2,1)}, bf16[128,1024]{1,0:T(8,128)(2,1)S(1)}, u32[]{:S(2)}, u32[]{:S(2)}) collective-permute-start(bf16[128,1024]{1,0:T(8,128)(2,1)} %collective-permute-done.4.refs_2_), channel_id=1, source_target_pairs={{0,1},{1,0},{2,3},{3,2},{4,5},{5,4},{6,7},{7,6},{8,9},{9,8},{10,11... | collective-permute-start | bytes 786440 | tf_op jit(solution)/shard_map/ppermute | solution.py:41
  40.9 2.9 %collective-permute-start.12 = (bf16[128,1024]{1,0:T(8,128)(2,1)S(1)}, bf16[128,1024]{1,0:T(8,128)(2,1)}, u32[]{:S(2)}, u32[]{:S(2)}) collective-permute-start(bf16[128,1024]{1,0:T(8,128)(2,1)S(1)} %conv1.1.refs_1_), channel_id=1, source_target_pairs={{0,1},{1,0},{2,3},{3,2},{4,5},{5,4},{6,7},{7,6},{8,9},{9,8},{10,11... | collective-permute-start | bytes 786440 | tf_op jit(solution)/shard_map/ppermute | solution.py:41
  41.4 2.4 %collective-permute-start.3 = (bf16[128,1024]{1,0:T(8,128)(2,1)S(1)}, bf16[128,1024]{1,0:T(8,128)(2,1)S(1)}, u32[]{:S(2)}, u32[]{:S(2)}) collective-permute-start(bf16[128,1024]{1,0:T(8,128)(2,1)S(1)} %conv3.1.refs_1_), channel_id=1, source_target_pairs={{0,1},{1,0},{2,3},{3,2},{4,5},{5,4},{6,7},{7,6},{8,9},{9,8},{10,11... | collective-permute-start | bytes 786440 | tf_op jit(solution)/shard_map/ppermute | solution.py:41
  41.5 8.8 %collective-permute-start.10 = (bf16[128,1024]{1,0:T(8,128)(2,1)S(1)}, bf16[128,1024]{1,0:T(8,128)(2,1)}, u32[]{:S(2)}, u32[]{:S(2)}) collective-permute-start(bf16[128,1024]{1,0:T(8,128)(2,1)S(1)} %conv2.1.refs_1_), channel_id=1, source_target_pairs={{0,2},{2,0},{1,3},{3,1},{4,6},{6,4},{5,7},{7,5},{8,10},{10,8},{9,1... | collective-permute-start | bytes 786440 | tf_op jit(solution)/shard_map/ppermute | solution.py:41
  42.6 7.9 %collective-permute-start.14 = (bf16[128,1024]{1,0:T(8,128)(2,1)}, bf16[128,1024]{1,0:T(8,128)(2,1)}, u32[]{:S(2)}, u32[]{:S(2)}) collective-permute-start(bf16[128,1024]{1,0:T(8,128)(2,1)} %collective-permute-done.13.refs_3_), channel_id=1, source_target_pairs={{0,1},{1,0},{2,3},{3,2},{4,5},{5,4},{6,7},{7,6},{8,9},{9,8},{10,11... | collective-permute-start | bytes 786440 | tf_op jit(solution)/shard_map/ppermute | solution.py:41
  43.3 37.5 %collective-permute-start.19 = (bf16[256,1024]{1,0:T(8,128)(2,1)S(1)}, bf16[256,1024]{1,0:T(8,128)(2,1)S(1)}, u32[]{:S(2)}, u32[]{:S(2)}) collective-permute-start(bf16[256,1024]{1,0:T(8,128)(2,1)S(1)} %copy-done.4), channel_id=1, source_target_pairs={{0,1},{1,0},{2,3},{3,2},{4,5},{5,4},{6,7},{7,6},{8,9},{9,8},{10,11... | collective-permute-start | bytes 1572872 | tf_op jit(solution)/shard_map/ppermute | solution.py:41
  43.8 22.7 %collective-permute-start.9 = (bf16[128,1024]{1,0:T(8,128)(2,1)S(1)}, bf16[128,1024]{1,0:T(8,128)(2,1)}, u32[]{:S(2)}, u32[]{:S(2)}) collective-permute-start(bf16[128,1024]{1,0:T(8,128)(2,1)S(1)} %conv2.1.refs_1_), channel_id=1, source_target_pairs={{0,1},{1,0},{2,3},{3,2},{4,5},{5,4},{6,7},{7,6},{8,9},{9,8},{10,11... | collective-permute-start | bytes 786440 | tf_op jit(solution)/shard_map/ppermute | solution.py:41
  43.9 22.5 %collective-permute-start.6 = (bf16[128,1024]{1,0:T(8,128)(2,1)}, bf16[128,1024]{1,0:T(8,128)(2,1)}, u32[]{:S(2)}, u32[]{:S(2)}) collective-permute-start(bf16[128,1024]{1,0:T(8,128)(2,1)} %copy-done.12), channel_id=1, source_target_pairs={{0,1},{1,0},{2,3},{3,2},{4,5},{5,4},{6,7},{7,6},{8,9},{9,8},{10,11... | collective-permute-start | bytes 786440 | tf_op jit(solution)/shard_map/ppermute | solution.py:41
  50.3 17.8 %collective-permute-start.11 = (bf16[128,1024]{1,0:T(8,128)(2,1)}, bf16[128,1024]{1,0:T(8,128)(2,1)}, u32[]{:S(2)}, u32[]{:S(2)}) collective-permute-start(bf16[128,1024]{1,0:T(8,128)(2,1)} %collective-permute-done.10.refs_3_), channel_id=1, source_target_pairs={{0,1},{1,0},{2,3},{3,2},{4,5},{5,4},{6,7},{7,6},{8,9},{9,8},{10,11... | collective-permute-start | bytes 786440 | tf_op jit(solution)/shard_map/ppermute | solution.py:41
  50.5 31.0 %collective-permute-start.24 = (bf16[16,16384]{1,0:T(8,128)(2,1)}, bf16[16,16384]{1,0:T(8,128)(2,1)S(1)}, u32[]{:S(2)}, u32[]{:S(2)}) collective-permute-start(bf16[16,16384]{1,0:T(8,128)(2,1)} %param.14), channel_id=1, source_target_pairs={{0,1},{1,0},{2,3},{3,2},{4,5},{5,4},{6,7},{7,6},{8,9},{9,8},{10,11... | collective-permute-start | bytes 1572872 | tf_op jit(solution)/shard_map/ppermute | solution.py:41
  66.4 15.5 %collective-permute-start.27 = (bf16[16,8192]{1,0:T(8,128)(2,1)S(1)}, bf16[16,8192]{1,0:T(8,128)(2,1)S(1)}, u32[]{:S(2)}, u32[]{:S(2)}) collective-permute-start(bf16[16,8192]{1,0:T(8,128)(2,1)S(1)} %collective-permute-done.25.refs_4_), channel_id=1, source_target_pairs={{0,1},{1,0},{2,3},{3,2},{4,5},{5,4},{6,7},{7,6},{8,9},{9,8},{10,11... | collective-permute-start | bytes 786440 | tf_op jit(solution)/shard_map/ppermute | solution.py:41
  66.5 14.9 %collective-permute-start.21 = (bf16[128,1024]{1,0:T(8,128)(2,1)S(1)}, bf16[128,1024]{1,0:T(8,128)(2,1)S(1)}, u32[]{:S(2)}, u32[]{:S(2)}) collective-permute-start(bf16[128,1024]{1,0:T(8,128)(2,1)S(1)} %collective-permute-done.20.refs_6_), channel_id=1, source_target_pairs={{0,16},{16,0},{1,17},{17,1},{2,18},{18,2},{3,19},{19,3},{4,20},{20... | collective-permute-start | bytes 786440 | tf_op jit(solution)/shard_map/ppermute | solution.py:41
  68.1 14.0 %collective-permute-start.28 = (bf16[16,8192]{1,0:T(8,128)(2,1)S(1)}, bf16[16,8192]{1,0:T(8,128)(2,1)S(1)}, u32[]{:S(2)}, u32[]{:S(2)}) collective-permute-start(bf16[16,8192]{1,0:T(8,128)(2,1)S(1)} %copy-done.6), channel_id=1, source_target_pairs={{0,1},{1,0},{2,3},{3,2},{4,5},{5,4},{6,7},{7,6},{8,9},{9,8},{10,11... | collective-permute-start | bytes 786440 | tf_op jit(solution)/shard_map/ppermute | solution.py:41
  80.9 1.8 %collective-permute-start.17 = (bf16[128,256]{1,0:T(8,128)(2,1)S(1)}, bf16[128,256]{1,0:T(8,128)(2,1)S(1)}, u32[]{:S(2)}, u32[]{:S(2)}) collective-permute-start(bf16[128,256]{1,0:T(8,128)(2,1)S(1)} %get-tuple-element.33), channel_id=1, source_target_pairs={{0,1},{1,0},{2,3},{3,2},{4,5},{5,4},{6,7},{7,6},{8,9},{9,8},{10,11... | collective-permute-start | bytes 196616 | tf_op jit(solution)/shard_map/ppermute | solution.py:41
  81.4 6.8 %collective-permute-start.22 = (bf16[128,1024]{1,0:T(8,128)(2,1)S(1)}, bf16[128,1024]{1,0:T(8,128)(2,1)S(1)}, u32[]{:S(2)}, u32[]{:S(2)}) collective-permute-start(bf16[128,1024]{1,0:T(8,128)(2,1)S(1)} %collective-permute-done.20.refs_6_), channel_id=1, source_target_pairs={{0,1},{1,0},{2,3},{3,2},{4,5},{5,4},{6,7},{7,6},{8,9},{9,8},{10,11... | collective-permute-start | bytes 786440 | tf_op jit(solution)/shard_map/ppermute | solution.py:41
  81.5 6.6 %collective-permute-start.23 = (bf16[128,1024]{1,0:T(8,128)(2,1)S(1)}, bf16[128,1024]{1,0:T(8,128)(2,1)S(1)}, u32[]{:S(2)}, u32[]{:S(2)}) collective-permute-start(bf16[128,1024]{1,0:T(8,128)(2,1)S(1)} %collective-permute-done.21.refs_7_), channel_id=1, source_target_pairs={{0,1},{1,0},{2,3},{3,2},{4,5},{5,4},{6,7},{7,6},{8,9},{9,8},{10,11... | collective-permute-start | bytes 786440 | tf_op jit(solution)/shard_map/ppermute | solution.py:41
  81.9 6.3 %collective-permute-start.15 = (bf16[128,256]{1,0:T(8,128)(2,1)S(1)}, bf16[128,256]{1,0:T(8,128)(2,1)S(1)}, u32[]{:S(2)}, u32[]{:S(2)}) collective-permute-start(bf16[128,256]{1,0:T(8,128)(2,1)S(1)} %get-tuple-element.31), channel_id=1, source_target_pairs={{0,1},{1,0},{2,3},{3,2},{4,5},{5,4},{6,7},{7,6},{8,9},{9,8},{10,11... | collective-permute-start | bytes 196616 | tf_op jit(solution)/shard_map/ppermute | solution.py:41
  82.0 6.1 %collective-permute-start.16 = (bf16[128,256]{1,0:T(8,128)(2,1)S(1)}, bf16[128,256]{1,0:T(8,128)(2,1)S(1)}, u32[]{:S(2)}, u32[]{:S(2)}) collective-permute-start(bf16[128,256]{1,0:T(8,128)(2,1)S(1)} %get-tuple-element.32), channel_id=1, source_target_pairs={{0,2},{2,0},{1,3},{3,1},{4,6},{6,4},{5,7},{7,5},{8,10},{10,8},{9,1... | collective-permute-start | bytes 196616 | tf_op jit(solution)/shard_map/ppermute | solution.py:41
  82.6 5.6 %collective-permute-start.18 = (bf16[128,256]{1,0:T(8,128)(2,1)S(1)}, bf16[128,256]{1,0:T(8,128)(2,1)S(1)}, u32[]{:S(2)}, u32[]{:S(2)}) collective-permute-start(bf16[128,256]{1,0:T(8,128)(2,1)S(1)} %collective-permute-done.17), channel_id=1, source_target_pairs={{0,2},{2,0},{1,3},{3,1},{4,6},{6,4},{5,7},{7,5},{8,10},{10,8},{9,1... | collective-permute-start | bytes 196616 | tf_op jit(solution)/shard_map/ppermute | solution.py:41
  (15 other events, 63.5 us)
